TPU v7x, 128 devices: a whole 4x4x4 slice. The times are simulated.
128 devices in a mesh: tm: 4 (over x), op: 32 (over y, z, core).
Axes of the slice: x: 4, y: 4, z: 4, core: 2. Of those that a mesh axis runs over, the one named last changes fastest.
Arguments:
- sink_elem: bfloat16 [2, 4, 2048, 16384], P(None, 'tm', 'op'), may hold values from -6 to 6
- source_elem: bfloat16 [2, 2, 2048, 16384], P(None, None, None, 'op'), may hold values from -6 to 6
- peram: bfloat16 [2, 4, 2, 512, 512], P(None, 'tm', None, 'op'), may hold values from -4 to 4
- pair_list: int32 [16, 1], replicated, may hold values from 0 to 15
- spin_sets: int32 [16, 3], replicated, may hold values from 0 to 3
Outputs:
- correlator: float32 [2, 4, 2, 16, 1], P(None, 'tm')
All inputs are finite; a program needn't handle non-finite values.
Results may differ from a plain program's by a relative error of at most 0.0041.
Values may be sent and summed in bfloat16 or wider, within the bound.
A program may use at most 192 MiB of HBM per device.

v0:
```python
import jax
import jax.numpy as jnp
from jax import lax
from jax.sharding import PartitionSpec as P

NEV = 128
NSPIN = 4
NOP = 16
TSRC = 2
PAIRS = 1


def complex_matrix(block):
    upper = jnp.concatenate([block[0], block[1]], axis=1)
    lower = jnp.concatenate([-block[1], block[0]], axis=1)
    return jnp.stack([upper, lower])


def on_device(sink_elem, source_elem, peram, pair_list, spin_sets):
    tau_all = lax.all_gather(peram, "op", axis=3, tiled=True)
    position = lax.axis_index("op")
    rows = sink_elem.shape[2]
    local_times = sink_elem.shape[1]
    span = min(rows, NEV)
    cols = source_elem.shape[3]

    def spin_block(local, t0, left, right):
        return lax.dynamic_slice(tau_all[:, local, t0], (0, left * NEV, right * NEV), (2, NEV, NEV))

    def sink_side(local, t0, p):
        op_now = (position * rows + 0) // NEV
        mine = spin_sets[op_now]
        theirs = spin_sets[pair_list[op_now, p]]
        third = complex_matrix(spin_block(local, t0, mine[2], theirs[2]))
        second = complex_matrix(spin_block(local, t0, mine[1], theirs[1]))
        phi = sink_elem[:, local, 0:span].reshape(2, span * NEV, NEV)
        x_both = jnp.einsum("cxk,ckb->xb", phi, third, preferred_element_type=jnp.float32)
        x_both = x_both.astype(jnp.bfloat16).reshape(span, NEV, 2, NEV)
        y_both = jnp.einsum("ijck,cjb->ibk", x_both, second, preferred_element_type=jnp.float32)
        y_both = y_both.astype(jnp.bfloat16).reshape(span, 2, NEV * NEV)
        pieces = jnp.transpose(y_both, (1, 0, 2))
        return pieces

    partial_terms = {}
    combos = [
        (local, t0, p) for local in range(local_times) for t0 in range(TSRC) for p in range(PAIRS)
    ]
    stacked = jnp.stack([sink_side(local, t0, p) for local, t0, p in combos], axis=1)
    columns = lax.all_to_all(stacked, "op", split_axis=3, concat_axis=2, tiled=True)
    for index, combo in enumerate(combos):
        column_t0 = combo[1]
        other = pair_list[:, combo[2]]
        source = source_elem[:, column_t0].reshape(2, NOP, NEV, cols)
        chosen = jnp.take(source, other, axis=1)
        tiles = columns[:, index].reshape(2, NOP, NEV, cols)

        def inner(a, b):
            return jnp.einsum("oic,ojc->oij", a, b, preferred_element_type=jnp.float32)

        m_re = inner(tiles[0], chosen[0]) + inner(tiles[1], chosen[1])
        m_im = inner(tiles[1], chosen[0]) - inner(tiles[0], chosen[1])
        blocks = tau_all[:, combo[0], column_t0].reshape(2, NSPIN, NEV, NSPIN, NEV)
        blocks = jnp.transpose(blocks, (1, 3, 0, 2, 4))
        first = blocks[spin_sets[:, 0], spin_sets[other, 0]].astype(jnp.float32)
        c_re = jnp.sum(first[:, 0] * m_re - first[:, 1] * m_im, axis=(1, 2))
        c_im = jnp.sum(first[:, 0] * m_im + first[:, 1] * m_re, axis=(1, 2))
        partial_terms[combo] = jnp.stack([c_re, c_im])
    local = 0
    per_time = []
    for t0 in range(TSRC):
        per_time.append(jnp.stack([partial_terms[local, t0, 0]], axis=-1))
    per_local = [jnp.stack(per_time, axis=1)]
    partial_sum = jnp.stack(per_local, axis=1)
    totals = lax.psum(partial_sum, "op")
    return totals * (1.0 / float(NEV**3))


def solution(mesh):
    in_specs = (
        P(None, "tm", "op", None),
        P(None, None, None, "op"),
        P(None, "tm", None, "op", None),
        P(),
        P(),
    )
    out_specs = P(None, "tm", None, None, None)
    return jax.shard_map(
        on_device, mesh=mesh, in_specs=in_specs, out_specs=out_specs, check_vma=False
    )
```

profile of v0, /device:TPU:1, one launch (start us, length us, event | category | flops | bytes accessed | tf_op | source)
XLA Modules:
  0.0 462.1 jit_solution(5356037397111504323)
XLA Ops:
  6.5 0.0 all-gather.2.cloned.1.call-start
  6.5 1.5 copy.40
  8.1 0.0 all-gather.2.cloned.1.call-update
  8.1 1.2 constant_dynamic-slice_fusion.1
  11.3 0.8 constant_dynamic-slice_fusion
  12.1 0.6 fusion.58
  15.2 7.4 %reshape_squeeze.19 = bf16[2,8192,128]{2,1,0:T(8,128)(2,1)} reshape(bf16[2,1,64,16384]{3,2,1,0:T(8,128)(2,1)} %param.7) | data formatting | bytes 8388608 | tf_op jit(solution)/shard_map/reshape;squeeze | solution.py:36
  22.6 34.7 %all-gather.2.cloned.1.call-done = bf16[2,1,2,512,512]{4,2,1,0,3:T(2,128)(2,1)} async-done(((bf16[2,1,2,16,512]{4,2,1,0,3:T(2,128)(2,1)}), bf16[2,1,2,512,512]{4,2,1,0,3:T(2,128)(2,1)}) %all-gather.2.cloned.1.call-update) | async-done | bytes 2097168 | tf_op jit(solution)/shard_map/all_gather | solution.py:20
  57.3 6.5 %fusion.57 = (bf16[2,1,1,512,512]{4,2,1,0,3:T(2,128)(2,1)}, bf16[2,1,1,512,512]{4,2,1,0,3:T(2,128)(2,1)S(1)}) fusion(bf16[2,1,2,512,512]{4,2,1,0,3:T(2,128)(2,1)} %all-gather.2.cloned.1.call-done), kind=kLoop, calls=%fused_computation.113 | loop fusion | bytes 4194304 | tf_op jit(solution)/shard_map/slice | solution.py:62
  63.8 4.6 copy.59
  68.4 4.2 copy.60
  72.6 0.8 dynamic-slice_bitcast_fusion.3
  73.4 0.8 fusion.53
  74.2 3.5 fusion.15
  77.7 1.2 copy.61
  78.9 7.4 %fusion.2 = bf16[64,256,128]{2,1,0:T(8,128)(2,1)} fusion(bf16[64,128,2,128]{1,0,3,2:T(8,128)(2,1)S(1)} %bitcast.218, bf16[1,128,256]{1,2,0:T(8,128)(2,1)S(1)} %get-tuple-element.35, bf16[1,128,256]{1,2,0:T(8,128)(2,1)S(1)} %get-tuple-element.34), kind=kOutput, calls=%fused_computation.12 | convolution fusion | flops 1076101120 | bytes 8519680 | tf_op jit(solution)/shard_map/ijck,cjb->ibk/dot_general | solution.py:39
  86.4 6.9 %reshape.75 = bf16[64,2,16384]{2,1,0:T(2,128)(2,1)} reshape(bf16[64,256,128]{2,1,0:T(8,128)(2,1)} %fusion.2) | data formatting | bytes 8388608 | tf_op jit(solution)/shard_map/reshape | solution.py:40
  93.2 6.6 %copy.83 = bf16[64,2,16384]{2,0,1:T(8,128)(2,1)} copy(bf16[64,2,16384]{2,1,0:T(2,128)(2,1)} %reshape.75) | data formatting | bytes 8388608 | tf_op jit(solution)/shard_map/reshape | solution.py:40
  99.9 0.0 copy-done.1
  99.9 1.3 fusion.14
  101.2 1.2 copy.62
  102.4 7.4 %fusion.3 = bf16[64,256,128]{2,1,0:T(8,128)(2,1)} fusion(bf16[64,128,2,128]{1,0,3,2:T(8,128)(2,1)S(1)} %bitcast.219, bf16[1,128,256]{1,2,0:T(8,128)(2,1)S(1)} %get-tuple-element.39, bf16[1,128,256]{1,2,0:T(8,128)(2,1)S(1)} %get-tuple-element.38), kind=kOutput, calls=%fused_computation.13 | convolution fusion | flops 1076101120 | bytes 8519680 | tf_op jit(solution)/shard_map/ijck,cjb->ibk/dot_general | solution.py:39
  109.8 6.9 %reshape.77 = bf16[64,2,16384]{2,1,0:T(2,128)(2,1)} reshape(bf16[64,256,128]{2,1,0:T(8,128)(2,1)} %fusion.3) | data formatting | bytes 8388608 | tf_op jit(solution)/shard_map/reshape | solution.py:40
  116.7 6.6 %copy.82 = bf16[64,2,16384]{2,0,1:T(8,128)(2,1)} copy(bf16[64,2,16384]{2,1,0:T(2,128)(2,1)} %reshape.77) | data formatting | bytes 8388608 | tf_op jit(solution)/shard_map/reshape | solution.py:40
  123.3 0.0 copy-done.4
  123.3 6.2 %pad_maximum_fusion = bf16[2,2,64,16384]{3,2,1,0:T(8,128)(2,1)} fusion(bf16[2,1,64,16384]{3,2,1,0:T(8,128)(2,1)} %bitcast.222, bf16[2,1,64,16384]{3,2,1,0:T(8,128)(2,1)S(1)} %bitcast.220), kind=kLoop, calls=%fused_computation.9 | loop fusion | flops 4194304 | bytes 16777216 | tf_op jit(solution)/shard_map/stack | solution.py:48
  129.5 34.5 %copy.49 = bf16[2,2,64,16384]{2,1,0,3:T(2,128)(2,1)} copy(bf16[2,2,64,16384]{3,2,1,0:T(8,128)(2,1)} %pad_maximum_fusion) | data formatting | bytes 16777216 | tf_op jit(solution)/shard_map/stack | solution.py:48
  164.0 26.7 %reshape.124 = bf16[32,2,65536]{2,1,0:T(2,128)(2,1)} reshape(bf16[16384,2,2,64]{3,2,1,0:T(2,128)(2,1)} %bitcast.211) | data formatting | bytes 16777216
  190.7 5.4 %all-to-all-start = ((bf16[32,2,65536]{2,1,0:T(2,128)(2,1)}), bf16[32,2,65536]{2,1,0:T(2,128)(2,1)}, u32[]{:S(2)}, u32[]{:S(2)}) async-start(bf16[32,2,65536]{2,1,0:T(2,128)(2,1)} %reshape.124), calls=%async_computation | async-start | bytes 16777216 | tf_op jit(solution)/shard_map/all_to_all | solution.py:49
  196.2 0.0 copy-done.8
  196.2 5.8 %fusion.56 = (bf16[2,1,2048,512]{3,2,1,0:T(8,128)(2,1)}, bf16[2,1,2048,512]{3,2,1,0:T(8,128)(2,1)}) fusion(bf16[2,2,2048,512]{3,2,1,0:T(8,128)(2,1)} %param.8), kind=kLoop, calls=%fused_computation.112 | loop fusion | bytes 16777216 | tf_op jit(solution)/shard_map/slice | solution.py:53
  202.0 5.0 %gather_fusion.3 = bf16[16,2,128,512]{3,2,1,0:T(8,128)(2,1)} fusion(bf16[2,16,128,512]{3,2,1,0:T(8,128)(2,1)} %bitcast.223, s32[1024]{0:T(1024)S(1)} %pad_clamp_fusion), kind=kCustom, calls=%fused_computation.clone | custom fusion | bytes 8388672 | tf_op jit(solution)/shard_map/jit(_take)/gather | solution.py:54
  207.0 5.0 %gather_fusion.4 = bf16[16,2,128,512]{3,2,1,0:T(8,128)(2,1)} fusion(bf16[2,16,128,512]{3,2,1,0:T(8,128)(2,1)} %bitcast.221, s32[1024]{0:T(1024)S(1)} %pad_clamp_fusion), kind=kCustom, calls=%fused_computation.1.clone | custom fusion | bytes 8388672 | tf_op jit(solution)/shard_map/jit(_take)/gather | solution.py:54
  211.9 0.0 copy-done
  212.0 0.7 gather_fusion
  212.7 0.0 copy-start.5
  212.7 6.0 %fusion.5 = (bf16[2,16,128,512]{3,2,1,0:T(8,128)(2,1)}, bf16[2,16,128,512]{3,2,1,0:T(8,128)(2,1)}) fusion(bf16[16,2,128,512]{3,2,1,0:T(8,128)(2,1)} %gather_fusion.3, pred[16]{0:T(512)(128)(4,1)S(1)} %compare_and_fusion, bf16[16,2,128,512]{3,2,1,0:T(8,128)(2,1)} %gather_fusion.4), kind=kLoop, calls=%fused_computation.17 | loop fusion | flops 4194304 | bytes 16777232 | tf_op jit(solution)/shard_map/jit(_take)/select_n | solution.py:54
  218.7 0.3 reshape_squeeze.18
  218.9 1.1 reshape_squeeze.21
  220.1 1.5 copy.42
  221.6 1.7 copy.52
  223.3 2.0 gather_fusion.1
  225.3 0.8 gather_fusion.2
  226.0 1.5 copy_convert_fusion.1
  227.6 1.6 copy_convert_fusion
  229.2 75.5 %all-to-all-done = bf16[32,2,65536]{2,1,0:T(2,128)(2,1)} async-done(((bf16[32,2,65536]{2,1,0:T(2,128)(2,1)}), bf16[32,2,65536]{2,1,0:T(2,128)(2,1)}, u32[]{:S(2)}, u32[]{:S(2)}) %all-to-all-start) | async-done | bytes 8388640 | tf_op jit(solution)/shard_map/all_to_all | solution.py:49
  304.7 26.0 %reshape.125 = bf16[16384,2,2,64]{3,2,1,0:T(2,128)(2,1)} reshape(bf16[32,2,65536]{2,1,0:T(2,128)(2,1)} %all-to-all-done) | data formatting | bytes 16777216
  330.7 36.1 %copy.50 = bf16[2,2,32,64,512]{4,3,2,1,0:T(8,128)(2,1)} copy(bf16[2,2,32,64,512]{3,1,0,4,2:T(2,128)(2,1)} %bitcast.212) | data formatting | bytes 16777216 | tf_op jit(solution)/shard_map/all_to_all | solution.py:49
  366.8 4.0 fusion.55
  370.8 0.7 copy-done.3
  371.4 0.7 fusion.17
  372.1 0.7 fusion.16
  372.8 0.0 copy-start.2
  372.9 0.8 fusion.26
  373.6 1.4 copy-done.2
  375.0 0.7 fusion.20
  375.7 0.7 fusion.21
  376.5 0.7 fusion.24
  377.2 0.9 copy-done.7
  378.0 0.8 subtract_reduce_fusion.1
  378.9 0.7 copy-done.6
  379.6 0.8 subtract_reduce_fusion
  380.5 74.2 %psum.7 = f32[2,1,2,16,1]{3,2,0,4,1:T(2,128)S(1)} all-reduce(f32[2,1,2,16,1]{3,2,0,4,1:T(2,128)S(1)} %bitcast.230), channel_id=1, replica_groups=mesh['tm'=4,'op'=32] {'op'}, use_global_device_ids=true, to_apply=%region_4.6 | all-reduce | flops 64 | bytes 512 | tf_op jit(solution)/shard_map/psum | solution.py:74
  454.7 0.6 broadcast_multiply_fusion
  (23 shorter events, 0.2 us)
Async XLA Ops:
  6.5 50.8 %all-gather.2.cloned.1.call-start = ((), (), s32[]{:S(2)}) async-start(), calls=%async_computation.1 | async-start | bytes 2162688 | tf_op jit(solution)/shard_map/all_gather | solution.py:20
  93.2 6.6 %copy-start.1 = (bf16[2,8192,128]{2,1,0:T(8,128)(2,1)S(1)}, bf16[2,8192,128]{2,1,0:T(8,128)(2,1)}, u32[]{:S(2)}) copy-start(bf16[2,8192,128]{2,1,0:T(8,128)(2,1)} %reshape_squeeze.19) | copy-start | bytes 12582916
  116.7 6.6 %copy-start.4 = (bf16[64,2,16384]{2,0,1:T(8,128)(2,1)S(1)}, bf16[64,2,16384]{2,0,1:T(8,128)(2,1)}, u32[]{:S(2)}) copy-start(bf16[64,2,16384]{2,0,1:T(8,128)(2,1)} %copy.83) | copy-start | bytes 12582916
  190.7 5.4 %copy-start.8 = (s32[16,1]{0,1:T(1,128)S(1)}, s32[16,1]{0,1:T(1,128)}, u32[]{:S(2)}) copy-start(s32[16,1]{0,1:T(1,128)} %param.10) | copy-start | bytes 196
  190.7 114.0 %all-to-all-start = ((bf16[32,2,65536]{2,1,0:T(2,128)(2,1)}), bf16[32,2,65536]{2,1,0:T(2,128)(2,1)}, u32[]{:S(2)}, u32[]{:S(2)}) async-start(bf16[32,2,65536]{2,1,0:T(2,128)(2,1)} %reshape.124), calls=%async_computation | async-start | bytes 16777216 | tf_op jit(solution)/shard_map/all_to_all | solution.py:49
  207.0 5.0 %copy-start = (s32[16,3]{0,1:T(4,128)S(1)}, s32[16,3]{0,1:T(4,128)}, u32[]{:S(2)}) copy-start(s32[16,3]{0,1:T(4,128)} %param.11) | copy-start | bytes 580
  212.7 6.3 %copy-start.5 = (bf16[2,1,1,512,512]{3,4,2,1,0:T(8,128)(2,1)S(1)}, bf16[2,1,1,512,512]{3,4,2,1,0:T(8,128)(2,1)}, u32[]{:S(2)}) copy-start(bf16[2,1,1,512,512]{3,4,2,1,0:T(8,128)(2,1)} %copy.60) | copy-start | bytes 3145732
  366.8 4.7 %copy-start.3 = (bf16[2,16,128,512]{3,2,1,0:T(8,128)(2,1)S(1)}, bf16[2,16,128,512]{3,2,1,0:T(8,128)(2,1)}, u32[]{:S(2)}) copy-start(bf16[2,16,128,512]{3,2,1,0:T(8,128)(2,1)} %get-tuple-element.48) | copy-start | bytes 12582916
  372.8 2.2 copy-start.2
  376.5 1.6 copy-start.7
  378.0 1.6 copy-start.6
Sparse Core Ops, SparseCore 0:
  9.6 47.6 all-gather.1
where the time goes:
time: 467 us; the launch traced here: 462 us
  local copies, waits for them, and re-layouts  212 us (45%)
  waiting for transfers between devices  110 us (24%)
  blocking collectives  74.2 us (16%)
  matrix products  25.6 us (5%)
  between operations  18.1 us (4%)
  other arithmetic  16.8 us (4%)
  starting transfers between devices  5.43 us (1%)
    all_to_all x1, waiting for transfers between devices, on_device(): lax.all_to_all(stacked, 'op', split_axis=3, concat_axis=2, tiled=True)  75.5 us
    psum x1, blocking collectives, on_device(): totals = lax.psum(partial_sum, 'op')  74.2 us
    unnamed x25, local copies, waits for them, and re-layouts  69.1 us
    all_to_all x1, local copies, waits for them, and re-layouts, on_device(): lax.all_to_all(stacked, 'op', split_axis=3, concat_axis=2, tiled=True)  36.1 us
    all_gather x1, waiting for transfers between devices, on_device(): tau_all = lax.all_gather(peram, 'op', axis=3, tiled=True)  34.7 us
    another operation x1, local copies, waits for them, and re-layouts, on_device(): jnp.stack([sink_side(local, t0, p) for local, t0, p in combos], axis=1)  34.5 us
    reshape x4, local copies, waits for them, and re-layouts, sink_side(): y_both = y_both.astype(jnp.bfloat16).reshape(span, 2, NEV * NEV)  27 us
    dot_general x2, matrix products, sink_side(): jnp.einsum('ijck,cjb->ibk', x_both, second, preferred_element_type=jnp.fl...  14.9 us
  transfers between devices with their start and end apart: 2, of which 2 were waited for; matrix products, arithmetic and copies ran while one was open for 9% of the time, Pallas kernels for 0%

commit v1 on v0

v1 whole, which is shorter than its diff:
```python
import functools

import jax
import jax.numpy as jnp
from jax import lax
from jax.experimental import pallas as pl
from jax.experimental.pallas import tpu as pltpu
from jax.sharding import PartitionSpec as P

NEV = 128
NOP = 16
TSRC = 2
MESH = pl.DeviceIdType.MESH
BF16 = jnp.bfloat16
F32 = jnp.float32

ORDER = [
    (0, 1), (1, 0), (0, 3), (3, 0), (1, 1), (3, 3), (1, 3), (3, 1),
    (2, 0), (0, 2), (2, 2), (1, 2), (2, 1), (3, 2), (2, 3),
]
PACKED_Y = sum(dy * 4**k for k, (dy, dz) in enumerate(ORDER))
PACKED_Z = sum(dz * 4**k for k, (dy, dz) in enumerate(ORDER))


def kernel(
    pair_ref, spin_ref, sink, source, peram, out,
    phi, sown, ssib, sbuf, rown, rnb, taub, xbuf, ybuf, pacc, t2m, t3m, mine, other, res,
    lsem, bsend, brecv, tsend, trecv, ssem, rsem, xsend, xrecv, fsend, frecv,
):
    t, o = lax.axis_index("tm"), lax.axis_index("op")
    h, chip = lax.rem(o, 2), lax.div(o, 2)
    y, z = lax.div(chip, 4), lax.rem(chip, 4)
    par = lax.rem(t, 2)
    sibling = (t, o + 1 - 2 * h)

    def at(y2, z2):
        return (t, (y2 * 4 + z2) * 2 + h)

    def beside(g):
        return (lax.rem(t + (1 - 2 * par) * (1 - 2 * g) + 4, 4), o)

    def remote(src, dst, send, recv, device):
        return pltpu.make_async_remote_copy(
            src_ref=src, dst_ref=dst, send_sem=send, recv_sem=recv, device_id=device, device_id_type=MESH
        )

    half = pl.ds(pl.multiple_of(par * 256, 256), 256)
    my_rows = pl.ds(pl.multiple_of(h * 64, 64), 64)

    local = []
    my_tau = pl.ds(pl.multiple_of(h * 16, 16), 16)
    for c in range(2):
        local.append(pltpu.make_async_copy(source.at[c, h, :, :, half], sown.at[c], lsem.at[c]))
    for c in range(2):
        local.append(pltpu.make_async_copy(sink.at[c, 0], phi.at[c, my_rows], lsem.at[2 + c]))
    for c in range(2):
        for b in range(4):
            local.append(
                pltpu.make_async_copy(
                    peram.at[c, 0, h, :, b * NEV : (b + 1) * NEV], taub.at[c, b, y, z, my_tau], lsem.at[4 + 4 * c + b]
                )
            )
    for copy in local:
        copy.start()

    barrier = pltpu.get_barrier_semaphore()

    def greet(k, carry):
        other_chip = lax.rem(chip + k, 16)
        pl.semaphore_signal(barrier, inc=1, device_id=(t, other_chip * 2 + h), device_id_type=MESH)
        return carry

    lax.fori_loop(1, 16, greet, 0)
    pl.semaphore_signal(barrier, inc=1, device_id=sibling, device_id_type=MESH)
    for g in range(2):
        pl.semaphore_signal(barrier, inc=1, device_id=beside(g), device_id_type=MESH)
    pl.semaphore_wait(barrier, 18)

    across = []
    for c in range(2):
        across.append(remote(source.at[c, 1 - h, :, :, half], ssib.at[c], bsend.at[c], brecv.at[c], sibling))
    for c in range(2):
        across.append(remote(sink.at[c, 0], phi.at[c, my_rows], bsend.at[2 + c], brecv.at[2 + c], sibling))
    for c in range(2):
        for b in range(4):
            n = 4 + 4 * c + b
            across.append(
                remote(
                    peram.at[c, 0, 1 - h, :, b * NEV : (b + 1) * NEV], taub.at[c, b, y, z, my_tau],
                    bsend.at[n], brecv.at[n], sibling,
                )
            )
    for copy in across[4:] + across[:4]:
        copy.start()

    for n in range(4, 12):
        local[n].wait()
        across[n].wait_recv()
    first, second = [], []
    for d in range(1, 4):
        y2, z2 = lax.rem(y + d, 4), lax.rem(z + d, 4)
        first.append(remote(taub.at[0, :, y, z], taub.at[0, :, y, z], tsend.at[d - 1], trecv.at[d - 1], at(y, z2)))
        first.append(remote(taub.at[1, :, y, z], taub.at[1, :, y, z], tsend.at[d + 2], trecv.at[d + 2], at(y2, z)))
        second.append(remote(taub.at[0, :, y], taub.at[0, :, y], tsend.at[d + 5], trecv.at[d + 5], at(y2, z)))
        second.append(remote(taub.at[1, :, :, z], taub.at[1, :, :, z], tsend.at[d + 8], trecv.at[d + 8], at(y, z2)))
    for copy in first:
        copy.start()

    def hand_on(slot, g):
        return remote(rown.at[slot], rnb.at[slot], xsend.at[slot], xrecv.at[slot], beside(g))

    def serve(p, tiles, g, begin, end, carry):
        def step(k, carry):
            cy, cz = carry
            target = lax.rem(y + lax.rem(cy, 4), 4) * 4 + lax.rem(z + lax.rem(cz, 4), 4)
            q = pair_ref[0, target]
            for c in range(2):
                sbuf[p * 15 + k, c] = tiles[c, q]
            send(p, k, target, g).start()
            return lax.div(cy, 4), lax.div(cz, 4)

        return lax.fori_loop(begin, end, step, carry)

    def send(p, k, target, g):
        return remote(
            sbuf.at[p * 15 + k], rown.at[chip * 2 + g], ssem.at[p * 15 + k], rsem.at[chip * 2 + g], (t, target * 2 + h)
        )

    def keep(tiles, g):
        q = pair_ref[0, chip]
        for c in range(2):
            rown[chip * 2 + g, c] = tiles[c, q]
        hand_on(chip * 2 + g, g).start()

    start = (jnp.int32(PACKED_Y), jnp.int32(PACKED_Z))
    for c in range(2):
        local[c].wait()
    carry = serve(0, sown, h, 0, 4, start)
    for copy in first:
        copy.wait_recv()
    for copy in second:
        copy.start()
    keep(sown, h)
    serve(0, sown, h, 4, 15, carry)
    for c in range(2):
        across[c].wait_recv()
    serve(1, ssib, 1 - h, 0, 15, start)
    keep(ssib, 1 - h)

    theirs = pair_ref[0, chip]
    for copy in second:
        copy.wait_recv()

    def block(c, n):
        left, right = spin_ref[n, chip], spin_ref[n, theirs]
        return taub[c, right, left].reshape(NEV, NEV)

    third_re, third_im = block(0, 2), block(1, 2)
    t3m[...] = jnp.concatenate(
        [jnp.concatenate([third_re, third_im], axis=1), jnp.concatenate([-third_im, third_re], axis=1)], axis=0
    )
    second_re, second_im = block(0, 1).astype(F32).T, block(1, 1).astype(F32).T
    t2m[...] = jnp.concatenate(
        [jnp.concatenate([second_re, -second_im], axis=1), jnp.concatenate([second_im, second_re], axis=1)], axis=0
    ).astype(BF16)
    for c in range(2):
        local[2 + c].wait()
        across[2 + c].wait_recv()

    def sender(carry):
        cy, cz = carry
        from_chip = lax.rem(y + 4 - lax.rem(cy, 4), 4) * 4 + lax.rem(z + 4 - lax.rem(cz, 4), 4)
        return from_chip, (lax.div(cy, 4), lax.div(cz, 4))

    def arrived(slot):
        remote(rown.at[slot], rown.at[slot], xsend.at[slot], rsem.at[slot], sibling).wait_recv()

    def take_and_hand_on(slot, g):
        arrived(slot)
        hand_on(slot, g).start()

    def rows16(ic, carry):
        i0 = pl.multiple_of(ic * 16, 16)

        def x_step(jb, inner):
            rows = []
            for jj in range(16):
                cols = pl.ds(pl.multiple_of((jb * 16 + jj) * NEV, NEV), NEV)
                rows.append(jnp.concatenate([phi[c, pl.ds(i0, 16), cols] for c in range(2)], axis=1))
            x = jnp.dot(jnp.concatenate(rows, axis=0), t3m[...], preferred_element_type=F32)
            place = pl.ds(pl.multiple_of(jb * 256, 256), 256)
            xbuf[0, place, :] = x[:, :NEV]
            xbuf[1, place, :] = x[:, NEV:]
            return inner

        lax.fori_loop(0, 8, x_step, 0)

        def y_step(ip, inner):
            parts = []
            for c in range(2):
                parts.append(
                    jnp.concatenate(
                        [xbuf[c, pl.ds(2 * ip + e, NEV, stride=16), :].astype(BF16) for e in range(2)], axis=1
                    )
                )
            value = jnp.dot(t2m[...], jnp.concatenate(parts, axis=0), preferred_element_type=F32)
            for e in range(2):
                place = pl.ds(pl.multiple_of((ic * 16 + 2 * ip + e) * 256, 256), 256)
                ybuf[place, :] = value[:, e * NEV : (e + 1) * NEV]
            return inner

        lax.fori_loop(0, 8, y_step, 0)
        for r in range(2):
            from_chip, later = sender(carry)
            slot = from_chip * 2 + h

            @pl.when(ic * 2 + r < 15)
            def _go():
                take_and_hand_on(slot, h)

            carry = later
        return carry

    lax.fori_loop(0, 8, rows16, start)

    pacc[...] = jnp.zeros_like(pacc)

    def contract(tile, slot, parity):
        first_j = slot * 4 + 2 * parity
        parts = []
        for c in range(2):
            parts.append(
                jnp.concatenate(
                    [ybuf[pl.ds(c * NEV + first_j + jj, NEV, stride=256), :].astype(BF16) for jj in range(2)], axis=1
                )
            )
        left = jnp.concatenate(parts, axis=0)
        right = tile[slot].reshape(2 * NEV, 256)
        pacc[...] += lax.dot_general(left, right, (((1,), (1,)), ((), ())), preferred_element_type=F32)

    def handed(slot):
        remote(rnb.at[slot], rnb.at[slot], xsend.at[slot], xrecv.at[slot], sibling).wait_recv()
        contract(rnb, slot, 1 - par)

    def main(k, carry):
        from_chip, carry = sender(carry)
        take_and_hand_on(from_chip * 2 + 1 - h, 1 - h)
        contract(rown, from_chip * 2 + h, par)
        contract(rown, from_chip * 2 + 1 - h, par)
        handed(from_chip * 2 + h)
        return carry

    contract(rown, chip * 2 + h, par)
    contract(rown, chip * 2 + 1 - h, par)
    lax.fori_loop(0, 15, main, start)
    handed(chip * 2 + h)
    handed(chip * 2 + 1 - h)

    def tail(k, carry):
        from_chip, carry = sender(carry)
        handed(from_chip * 2 + 1 - h)
        return carry

    lax.fori_loop(0, 15, tail, start)

    first_re, first_im = block(0, 0).astype(F32), block(1, 0).astype(F32)
    m_re = pacc[:NEV, :NEV] + pacc[NEV:, NEV:]
    m_im = pacc[NEV:, :NEV] - pacc[:NEV, NEV:]

    def total(v):
        return jnp.sum(jnp.sum(v, axis=0, keepdims=True), axis=1, keepdims=True) * (1.0 / float(NEV**3))

    c_re, c_im = total(first_re * m_re - first_im * m_im), total(first_re * m_im + first_im * m_re)
    row = lax.broadcasted_iota(jnp.int32, (8, NEV), 0)
    zero = jnp.zeros((8, NEV), F32)
    mine[...] = jnp.where(row == h, zero + c_re, jnp.where(row == 2 + h, zero + c_im, zero))
    swap = remote(mine, other, fsend.at[15], frecv.at[16], sibling)
    swap.start()
    swap.wait()
    res[chip] = mine[...] + other[...]

    def share(k):
        target = lax.rem(chip + k, 16)
        return remote(res.at[chip], res.at[chip], fsend.at[k - 1], frecv.at[chip], (t, target * 2 + h))

    def share_start(k, carry):
        share(k).start()
        return carry

    lax.fori_loop(1, 16, share_start, 0)

    def share_wait(k, carry):
        who = lax.rem(chip + k, 16)
        share(k).wait_send()
        remote(res.at[who], res.at[who], fsend.at[k - 1], frecv.at[who], sibling).wait_recv()
        return carry

    lax.fori_loop(1, 16, share_wait, 0)
    lane = lax.broadcasted_iota(jnp.int32, (8, NEV), 1)
    gathered = zero
    for n in range(NOP):
        gathered = jnp.where(lane == n, res[n], gathered)
    out[...] = gathered

    for copy in across + first + second:
        copy.wait_send()

    def drain_sends(k, carry):
        remote(sbuf.at[k], sbuf.at[k], ssem.at[k], xrecv.at[0], sibling).wait_send()
        return carry

    lax.fori_loop(0, 30, drain_sends, 0)

    def drain_hands(k, carry):
        remote(rown.at[k], rown.at[k], xsend.at[k], xrecv.at[0], sibling).wait_send()
        return carry

    lax.fori_loop(0, 32, drain_hands, 0)


def on_device(sink_elem, source_elem, peram, pair_list, spin_sets):
    gathered = pl.pallas_call(
        kernel,
        name="correlate",
        out_shape=jax.ShapeDtypeStruct((8, NEV), F32),
        in_specs=[
            pl.BlockSpec(memory_space=pltpu.SMEM),
            pl.BlockSpec(memory_space=pltpu.SMEM),
            pl.BlockSpec(memory_space=pl.ANY),
            pl.BlockSpec(memory_space=pl.ANY),
            pl.BlockSpec(memory_space=pl.ANY),
        ],
        out_specs=pl.BlockSpec(memory_space=pltpu.VMEM),
        scratch_shapes=[
            pltpu.VMEM((2, NEV, NEV * NEV), BF16),
            pltpu.VMEM((2, NOP, NEV, 256), BF16),
            pltpu.VMEM((2, NOP, NEV, 256), BF16),
            pltpu.VMEM((30, 2, NEV, 256), BF16),
            pltpu.VMEM((32, 2, NEV, 256), BF16),
            pltpu.VMEM((32, 2, NEV, 256), BF16),
            pltpu.VMEM((2, 4, 4, 4, 32, NEV), BF16),
            pltpu.VMEM((2, 16 * NEV, NEV), F32),
            pltpu.VMEM((2 * NEV * NEV, NEV), F32),
            pltpu.VMEM((2 * NEV, 2 * NEV), F32),
            pltpu.VMEM((2 * NEV, 2 * NEV), BF16),
            pltpu.VMEM((2 * NEV, 2 * NEV), BF16),
            pltpu.VMEM((8, NEV), F32),
            pltpu.VMEM((8, NEV), F32),
            pltpu.VMEM((NOP, 8, NEV), F32),
            pltpu.SemaphoreType.DMA((12,)),
            pltpu.SemaphoreType.DMA((12,)),
            pltpu.SemaphoreType.DMA((12,)),
            pltpu.SemaphoreType.DMA((12,)),
            pltpu.SemaphoreType.DMA((12,)),
            pltpu.SemaphoreType.DMA((30,)),
            pltpu.SemaphoreType.DMA((32,)),
            pltpu.SemaphoreType.DMA((32,)),
            pltpu.SemaphoreType.DMA((32,)),
            pltpu.SemaphoreType.DMA((16,)),
            pltpu.SemaphoreType.DMA((17,)),
        ],
        compiler_params=pltpu.CompilerParams(
            collective_id=0, has_side_effects=True, vmem_limit_bytes=56 * 2**20
        ),
    )(pair_list.T, spin_sets.T, sink_elem, source_elem.reshape(2, TSRC, NOP, NEV, source_elem.shape[3]), peram)
    return gathered[:4, :NOP].reshape(2, 1, TSRC, NOP, 1)


def solution(mesh):
    in_specs = (
        P(None, "tm", "op", None),
        P(None, None, None, "op"),
        P(None, "tm", None, "op", None),
        P(),
        P(),
    )
    out_specs = P(None, "tm", None, None, None)
    return jax.shard_map(on_device, mesh=mesh, in_specs=in_specs, out_specs=out_specs, check_vma=False)
```

time: 467 us -> 91.6 us (0.20); the launches traced: 462 us -> 91.4 us
  local copies, waits for them, and re-layouts: 212 us -> 1.26 us
  waiting for transfers between devices: 110 us -> 0 us
  Pallas kernels: 0 us -> 90.1 us
  blocking collectives: 74.2 us -> 0 us
  matrix products: 25.6 us -> 0 us
  between operations: 18.1 us -> 0.01 us
  other arithmetic: 16.8 us -> 0 us
  starting transfers between devices: 5.43 us -> 0 us
    pallas_call x0 -> x1, Pallas kernels: none -> 90.1 us  [on_device(): pl.pallas_call(kernel, name='correlate', out_shape=jax.ShapeDtypeStruct((...]
    all_to_all x1 -> x0, waiting for transfers between devices: 75.5 us -> none  [on_device(): lax.all_to_all(stacked, 'op', split_axis=3, concat_axis=2, tiled=True)]
    psum x1 -> x0, blocking collectives: 74.2 us -> none  [on_device(): totals = lax.psum(partial_sum, 'op')]
    unnamed x25 -> x0, local copies, waits for them, and re-layouts: 69.1 us -> none
    another operation x7 -> x0, local copies, waits for them, and re-layouts: 46.5 us -> none  [the longest x1 34.5 us: on_device(): jnp.stack([sink_side(local, t0, p) for local, t0, p in combos], axis=1)]
    all_to_all x1 -> x0, local copies, waits for them, and re-layouts: 36.1 us -> none  [on_device(): lax.all_to_all(stacked, 'op', split_axis=3, concat_axis=2, tiled=True)]
    all_gather x1 -> x0, waiting for transfers between devices: 34.7 us -> none  [on_device(): tau_all = lax.all_gather(peram, 'op', axis=3, tiled=True)]
    reshape x4 -> x0, local copies, waits for them, and re-layouts: 27 us -> none  [sink_side(): y_both = y_both.astype(jnp.bfloat16).reshape(span, 2, NEV * NEV)]
  transfers between devices with their start and end apart: 2 -> 0, of which waited for: 2 -> 0; matrix products, arithmetic and copies ran while one was open for 9% -> 0% of each run, Pallas kernels for 0% -> 0%
where the time goes in v1:
time: 91.6 us; the launch traced here: 91.4 us
  Pallas kernels  90.1 us (98%)
  local copies, waits for them, and re-layouts  1.26 us (1%)
    pallas_call x1, Pallas kernels, on_device(): pl.pallas_call(kernel, name='correlate', out_shape=jax.ShapeDtypeStruct((...  90.1 us

profile of v1, /device:TPU:1, one launch (start us, length us, event | category | flops | bytes accessed | tf_op | source)
XLA Modules:
  0.0 91.4 jit_solution(10826706711095857705)
XLA Ops:
  0.0 90.1 %correlate.1 = f32[8,128]{1,0:T(8,128)} custom-call(s32[1,16]{1,0:T(1,128)} %bitcast.8, s32[3,16]{1,0:T(4,128)} %bitcast.7, bf16[2,1,64,16384]{3,2,1,0:T(8,128)(2,1)} %sink.1, bf16[2,2,16,128,512]{4,3,2,1,0:T(8,128)(2,1)} %bitcast.6, bf16[2,1,2,16,512]{4,3,2,1,0:T(8,128)(2,1)} %peram.1), custom_call_target="tpu_custom_call" | custom-call | tf_op jit(solution)/shard_map/correlate/pallas_call | solution.py:322
  90.2 1.3 %slice.3 = f32[4,16]{1,0:T(4,128)} slice(f32[8,128]{1,0:T(8,128)} %correlate.1), slice={[0:4], [0:16]} | slice | bytes 512 | tf_op jit(solution)/shard_map/slice | solution.py:366

commit v2 on v1

v2 whole, which is shorter than its diff:
```python
import functools

import jax
import jax.numpy as jnp
from jax import lax
from jax.experimental import pallas as pl
from jax.experimental.pallas import tpu as pltpu
from jax.sharding import PartitionSpec as P

NEV = 128
NOP = 16
TSRC = 2
MESH = pl.DeviceIdType.MESH
BF16 = jnp.bfloat16
F32 = jnp.float32

XJ = 64
YP = 4
OUT = 12
EARLY = (4, 4)

ORDER = [
    (0, 1), (1, 0), (0, 3), (3, 0), (1, 1), (3, 3), (1, 3), (3, 1),
    (2, 0), (0, 2), (2, 2), (1, 2), (2, 1), (3, 2), (2, 3),
]
PACKED_Y = sum(dy * 4**k for k, (dy, dz) in enumerate(ORDER))
PACKED_Z = sum(dz * 4**k for k, (dy, dz) in enumerate(ORDER))


def kernel(
    pair_ref, spin_ref, sink, source, peram, out,
    phi, sown, ssib, sbuf, rown, rnb, taub, tout, tsel, xbuf, ybuf, pacc, t2m, t3m, mine, other, res,
    lsem, bsend, brecv, tsend, trecv, ssem, rsem, xsend, xrecv, fsend, frecv,
):
    t, o = lax.axis_index("tm"), lax.axis_index("op")
    h, chip = lax.rem(o, 2), lax.div(o, 2)
    y, z = lax.div(chip, 4), lax.rem(chip, 4)
    par = lax.rem(t, 2)
    sibling = (t, o + 1 - 2 * h)

    def at(y2, z2):
        return (t, (y2 * 4 + z2) * 2 + h)

    def beside(g):
        return (lax.rem(t + (1 - 2 * par) * (1 - 2 * g) + 4, 4), o)

    def remote(src, dst, send, recv, device):
        return pltpu.make_async_remote_copy(
            src_ref=src, dst_ref=dst, send_sem=send, recv_sem=recv, device_id=device, device_id_type=MESH
        )

    my_rows = pl.ds(pl.multiple_of(h * 64, 64), 64)

    local = []
    my_tau = pl.ds(pl.multiple_of(h * 16, 16), 16)
    for c in range(2):
        some = pl.ds(c * 8, 8)
        local.append(pltpu.make_async_copy(source.at[par, h, some], sown.at[some], lsem.at[c]))
    for c in range(2):
        local.append(pltpu.make_async_copy(sink.at[c, 0], phi.at[c, my_rows], lsem.at[2 + c]))
    for c in range(2):
        for b in range(4):
            local.append(
                pltpu.make_async_copy(
                    peram.at[c, 0, h, :, b * NEV : (b + 1) * NEV], taub.at[c, b, y, my_tau], lsem.at[4 + 4 * c + b]
                )
            )
    for copy in local:
        copy.start()

    barrier = pltpu.get_barrier_semaphore()

    def greet(k, carry):
        other_chip = lax.rem(chip + k, 16)
        pl.semaphore_signal(barrier, inc=1, device_id=(t, other_chip * 2 + h), device_id_type=MESH)
        return carry

    lax.fori_loop(1, 16, greet, 0)
    pl.semaphore_signal(barrier, inc=1, device_id=sibling, device_id_type=MESH)
    for g in range(2):
        pl.semaphore_signal(barrier, inc=1, device_id=beside(g), device_id_type=MESH)
    pl.semaphore_wait(barrier, 18)

    across = []
    for c in range(2):
        some = pl.ds(c * 8, 8)
        across.append(remote(source.at[par, 1 - h, some], ssib.at[some], bsend.at[c], brecv.at[c], sibling))
    for c in range(2):
        across.append(remote(sink.at[c, 0], phi.at[c, my_rows], bsend.at[2 + c], brecv.at[2 + c], sibling))
    for c in range(2):
        for b in range(4):
            n = 4 + 4 * c + b
            across.append(
                remote(
                    peram.at[c, 0, 1 - h, :, b * NEV : (b + 1) * NEV], taub.at[c, b, y, my_tau],
                    bsend.at[n], brecv.at[n], sibling,
                )
            )
    for copy in across[4:] + across[:4]:
        copy.start()

    first, second = [], []
    for d in range(1, 4):
        y2, z2 = lax.rem(y + d, 4), lax.rem(z + d, 4)
        first.append(remote(taub.at[:, :, y], taub.at[:, :, y], tsend.at[d - 1], trecv.at[d - 1], at(y2, z)))
        second.append(remote(tout.at[d - 1], tsel.at[:, :, z], tsend.at[d + 2], trecv.at[d + 2], at(y, z2)))

    def spread_rows():
        for n in range(4, 12):
            local[n].wait()
            across[n].wait_recv()
        for copy in first:
            copy.start()

    def pick(d, n, c):
        target = y * 4 + lax.rem(z + d, 4)
        return taub[c, spin_ref[n, pair_ref[0, target]], spin_ref[n, target]]

    def spread_blocks():
        for copy in first:
            copy.wait_recv()
        for d in range(1, 4):
            for n in range(3):
                for c in range(2):
                    tout[d - 1, n, c] = pick(d, n, c)
            second[d - 1].start()
        for n in range(3):
            for c in range(2):
                tsel[n, c, z] = pick(0, n, c)

    def hand_on(slot, g):
        return remote(rown.at[slot], rnb.at[slot], xsend.at[slot], xrecv.at[slot], beside(g))

    def advance(order):
        return tuple(lax.div(digits, 4) + lax.rem(digits, 4) * 4**14 for digits in order)

    def half_of(m):
        return lax.rem(h + lax.div(m, 15), 2)

    def serve(m, order):
        target = lax.rem(y + lax.rem(order[0], 4), 4) * 4 + lax.rem(z + lax.rem(order[1], 4), 4)
        q = pair_ref[0, target]

        @pl.when(m < 15)
        def _own():
            sbuf[m] = sown[q]

        @pl.when(m >= 15)
        def _sib():
            sbuf[m] = ssib[q]

        place = chip * 2 + half_of(m)
        remote(sbuf.at[m], rown.at[place], ssem.at[m], rsem.at[place], (t, target * 2 + h)).start()
        return advance(order)

    def keep(p, tiles):
        q = pair_ref[0, chip]
        g = lax.rem(h + p, 2)
        rown[chip * 2 + g] = tiles[q]
        hand_on(chip * 2 + g, g).start()

    def slot_of(m, order):
        from_y, from_z = lax.rem(y + 4 - lax.rem(order[0], 4), 4), lax.rem(z + 4 - lax.rem(order[1], 4), 4)
        return (from_y * 4 + from_z) * 2 + half_of(m)

    def pump(n, orders):
        coming, going = orders
        slot = slot_of(n, coming)
        remote(rown.at[slot], rown.at[slot], xsend.at[slot], rsem.at[slot], sibling).wait_recv()
        hand_on(slot, half_of(n)).start()

        @pl.when(n < 30 - OUT)
        def _more():
            serve(n + OUT, going)

        return advance(coming), advance(going)

    start = (jnp.int32(PACKED_Y), jnp.int32(PACKED_Z))
    for c in range(2):
        local[c].wait()
    keep(0, sown)
    going = lax.fori_loop(0, OUT, serve, start)
    spread_rows()
    for c in range(2):
        across[c].wait_recv()
    keep(1, ssib)
    orders = lax.fori_loop(0, EARLY[0], pump, (start, going))
    spread_blocks()
    orders = lax.fori_loop(EARLY[0], EARLY[0] + EARLY[1], pump, orders)

    for copy in second:
        copy.wait_recv()

    def block(c, n):
        return tsel[n, c].reshape(NEV, NEV)

    third_re, third_im = block(0, 2), block(1, 2)
    t3m[...] = jnp.concatenate(
        [jnp.concatenate([third_re, third_im], axis=1), jnp.concatenate([-third_im, third_re], axis=1)], axis=0
    )
    second_re, second_im = block(0, 1).astype(F32).T, block(1, 1).astype(F32).T
    t2m[...] = jnp.concatenate(
        [jnp.concatenate([second_re, -second_im], axis=1), jnp.concatenate([second_im, second_re], axis=1)], axis=0
    ).astype(BF16)
    for c in range(2):
        local[2 + c].wait()
        across[2 + c].wait_recv()

    def rows16(ic, orders):
        n = EARLY[0] + EARLY[1] + ic * 2
        i0 = pl.multiple_of(ic * 16, 16)

        def x_step(jb, inner):
            rows = []
            for jj in range(XJ):
                cols = pl.ds(pl.multiple_of((jb * XJ + jj) * NEV, NEV), NEV)
                rows.append(jnp.concatenate([phi[c, pl.ds(i0, 16), cols] for c in range(2)], axis=1))
            x = jnp.dot(jnp.concatenate(rows, axis=0), t3m[...], preferred_element_type=F32)
            place = pl.ds(pl.multiple_of(jb * (XJ * 16), XJ * 16), XJ * 16)
            xbuf[0, place, :] = x[:, :NEV]
            xbuf[1, place, :] = x[:, NEV:]
            return inner

        lax.fori_loop(0, NEV // XJ, x_step, 0)
        orders = pump(n, orders)

        def y_step(iq, inner):
            for ip in range(YP):
                first_i = iq * (2 * YP) + 2 * ip
                parts = []
                for c in range(2):
                    parts.append(
                        jnp.concatenate(
                            [xbuf[c, pl.ds(first_i + e, NEV, stride=16), :].astype(BF16) for e in range(2)], axis=1
                        )
                    )
                value = jnp.dot(t2m[...], jnp.concatenate(parts, axis=0), preferred_element_type=F32)
                for e in range(2):
                    place = pl.ds(pl.multiple_of((ic * 16 + first_i + e) * 256, 256), 256)
                    ybuf[place, :] = value[:, e * NEV : (e + 1) * NEV]
            return inner

        lax.fori_loop(0, 8 // YP, y_step, 0)
        return pump(n + 1, orders)

    orders = lax.fori_loop(0, 8, rows16, orders)

    def contract(slots):
        left, right = [[], []], [[], []]
        for slot in slots:
            for c in range(2):
                for jj in range(4):
                    left[c].append(ybuf[pl.ds(c * NEV + slot * 4 + jj, NEV, stride=256), :].astype(BF16))
            right[0].append(rown[slot])
            right[1].append(rnb[slot])
        left, right = (
            jnp.concatenate([jnp.concatenate(part, axis=1) for part in parts], axis=0) for parts in (left, right)
        )
        return lax.dot_general(left, right, (((1,), (1,)), ((), ())), preferred_element_type=F32)

    def handed(slot):
        remote(rnb.at[slot], rnb.at[slot], xsend.at[slot], xrecv.at[slot], sibling).wait_recv()

    own, nxt = chip * 2 + h, chip * 2 + 1 - h
    handed(own)
    handed(nxt)
    pacc[...] = contract([own, nxt])

    def main(k, carry):
        orders, order = carry
        n = EARLY[0] + EARLY[1] + 16 + k

        @pl.when(n < 30)
        def _last():
            pump(n, orders)

        a, order = slot_of(2 * k, order), advance(order)
        b, order = slot_of(2 * k + 1, order), advance(order)
        handed(a)
        handed(b)
        pacc[...] += contract([a, b])
        return (advance(orders[0]), advance(orders[1])), order

    lax.fori_loop(0, 15, main, (orders, start))

    for copy in across + first + second:
        copy.wait_send()

    def drain_sends(k, inner):
        remote(sbuf.at[k], sbuf.at[k], ssem.at[k], xrecv.at[0], sibling).wait_send()
        return inner

    lax.fori_loop(0, 30, drain_sends, 0)

    first_re, first_im = block(0, 0).astype(F32), block(1, 0).astype(F32)
    fetched, given = pacc[:, :NEV], pacc[:, NEV:]
    with_re, with_im = jnp.where(par == 0, fetched, given), jnp.where(par == 0, given, fetched)
    m_re = with_re[:NEV] + with_im[NEV:]
    m_im = with_re[NEV:] - with_im[:NEV]

    def total(v):
        return jnp.sum(jnp.sum(v, axis=0, keepdims=True), axis=1, keepdims=True) * (1.0 / float(NEV**3))

    c_re, c_im = total(first_re * m_re - first_im * m_im), total(first_re * m_im + first_im * m_re)
    row = lax.broadcasted_iota(jnp.int32, (8, NEV), 0)
    zero = jnp.zeros((8, NEV), F32)
    mine[...] = jnp.where(row == h, zero + c_re, jnp.where(row == 2 + h, zero + c_im, zero))
    swap = remote(mine, other, fsend.at[15], frecv.at[16], sibling)
    swap.start()
    swap.wait()
    res[chip] = mine[...] + other[...]

    def share(k):
        target = lax.rem(chip + k, 16)
        return remote(res.at[chip], res.at[chip], fsend.at[k - 1], frecv.at[chip], (t, target * 2 + h))

    def share_start(k, carry):
        share(k).start()
        return carry

    lax.fori_loop(1, 16, share_start, 0)

    def drain_hands(k, carry):
        remote(rown.at[k], rown.at[k], xsend.at[k], xrecv.at[0], sibling).wait_send()
        return carry

    lax.fori_loop(0, 32, drain_hands, 0)

    def share_wait(k, carry):
        who = lax.rem(chip + k, 16)
        share(k).wait_send()
        remote(res.at[who], res.at[who], fsend.at[k - 1], frecv.at[who], sibling).wait_recv()
        return carry

    lax.fori_loop(1, 16, share_wait, 0)
    lane = lax.broadcasted_iota(jnp.int32, (8, NEV), 1)
    gathered = zero
    for n in range(NOP):
        gathered = jnp.where(lane == n, res[n], gathered)
    out[...] = gathered


def on_device(sink_elem, source_elem, peram, pair_list, spin_sets):
    gathered = pl.pallas_call(
        kernel,
        name="correlate",
        out_shape=jax.ShapeDtypeStruct((8, NEV), F32),
        in_specs=[
            pl.BlockSpec(memory_space=pltpu.SMEM),
            pl.BlockSpec(memory_space=pltpu.SMEM),
            pl.BlockSpec(memory_space=pl.ANY),
            pl.BlockSpec(memory_space=pl.ANY),
            pl.BlockSpec(memory_space=pl.ANY),
        ],
        out_specs=pl.BlockSpec(memory_space=pltpu.VMEM),
        scratch_shapes=[
            pltpu.VMEM((2, NEV, NEV * NEV), BF16),
            pltpu.VMEM((NOP, NEV, 512), BF16),
            pltpu.VMEM((NOP, NEV, 512), BF16),
            pltpu.VMEM((30, NEV, 512), BF16),
            pltpu.VMEM((32, NEV, 512), BF16),
            pltpu.VMEM((32, NEV, 512), BF16),
            pltpu.VMEM((2, 4, 4, 32, NEV), BF16),
            pltpu.VMEM((3, 3, 2, 32, NEV), BF16),
            pltpu.VMEM((3, 2, 4, 32, NEV), BF16),
            pltpu.VMEM((2, 16 * NEV, NEV), F32),
            pltpu.VMEM((2 * NEV * NEV, NEV), F32),
            pltpu.VMEM((2 * NEV, 2 * NEV), F32),
            pltpu.VMEM((2 * NEV, 2 * NEV), BF16),
            pltpu.VMEM((2 * NEV, 2 * NEV), BF16),
            pltpu.VMEM((8, NEV), F32),
            pltpu.VMEM((8, NEV), F32),
            pltpu.VMEM((NOP, 8, NEV), F32),
            pltpu.SemaphoreType.DMA((12,)),
            pltpu.SemaphoreType.DMA((12,)),
            pltpu.SemaphoreType.DMA((12,)),
            pltpu.SemaphoreType.DMA((12,)),
            pltpu.SemaphoreType.DMA((12,)),
            pltpu.SemaphoreType.DMA((30,)),
            pltpu.SemaphoreType.DMA((32,)),
            pltpu.SemaphoreType.DMA((32,)),
            pltpu.SemaphoreType.DMA((32,)),
            pltpu.SemaphoreType.DMA((16,)),
            pltpu.SemaphoreType.DMA((17,)),
        ],
        compiler_params=pltpu.CompilerParams(
            collective_id=0, has_side_effects=True, vmem_limit_bytes=56 * 2**20
        ),
    )(pair_list.T, spin_sets.T, sink_elem, source_elem.reshape(2, TSRC, NOP, NEV, source_elem.shape[3]), peram)
    return gathered[:4, :NOP].reshape(2, 1, TSRC, NOP, 1)


def solution(mesh):
    in_specs = (
        P(None, "tm", "op", None),
        P(None, None, None, "op"),
        P(None, "tm", None, "op", None),
        P(),
        P(),
    )
    out_specs = P(None, "tm", None, None, None)
    return jax.shard_map(on_device, mesh=mesh, in_specs=in_specs, out_specs=out_specs, check_vma=False)
```

time: 91.6 us -> 85 us (0.928)
  Pallas kernels: 90.1 us -> 83.6 us
    pallas_call x1, Pallas kernels: 90.1 us -> 83.6 us  [on_device(): pl.pallas_call(kernel, name='correlate', out_shape=jax.ShapeDtypeStruct((...]
where the time goes in v2:
time: 85 us; the launch traced here: 84.8 us
  Pallas kernels  83.6 us (98%)
  local copies, waits for them, and re-layouts  1.26 us (1%)
    pallas_call x1, Pallas kernels, on_device(): pl.pallas_call(kernel, name='correlate', out_shape=jax.ShapeDtypeStruct((...  83.6 us

profile of v2, /device:TPU:1, one launch (start us, length us, event | category | flops | bytes accessed | tf_op | source)
XLA Modules:
  0.0 84.8 jit_solution(7175808610322835895)
XLA Ops:
  0.0 83.6 %correlate.1 = f32[8,128]{1,0:T(8,128)} custom-call(s32[1,16]{1,0:T(1,128)} %bitcast.8, s32[3,16]{1,0:T(4,128)} %bitcast.7, bf16[2,1,64,16384]{3,2,1,0:T(8,128)(2,1)} %sink.1, bf16[2,2,16,128,512]{4,3,2,1,0:T(8,128)(2,1)} %bitcast.6, bf16[2,1,2,16,512]{4,3,2,1,0:T(8,128)(2,1)} %peram.1), custom_call_target="tpu_custom_call" | custom-call | tf_op jit(solution)/shard_map/correlate/pallas_call | solution.py:344
  83.6 1.3 %slice.3 = f32[4,16]{1,0:T(4,128)} slice(f32[8,128]{1,0:T(8,128)} %correlate.1), slice={[0:4], [0:16]} | slice | bytes 512 | tf_op jit(solution)/shard_map/slice | solution.py:390

commit v3 on v2

--- a/solution.py
+++ b/solution.py
@@ -17,7 +17,7 @@
 XJ = 64
 YP = 4
 OUT = 12
-EARLY = (4, 4)
+EARLY = (4, 6)
 
 ORDER = [
     (0, 1), (1, 0), (0, 3), (3, 0), (1, 1), (3, 3), (1, 3), (3, 1),
@@ -62,7 +62,7 @@
         for b in range(4):
             local.append(
                 pltpu.make_async_copy(
-                    peram.at[c, 0, h, :, b * NEV : (b + 1) * NEV], taub.at[c, b, y, my_tau], lsem.at[4 + 4 * c + b]
+                    peram.at[c, 0, h, :, b * NEV : (b + 1) * NEV], taub.at[y, c, b, my_tau], lsem.at[4 + 4 * c + b]
                 )
             )
     for copy in local:
@@ -92,7 +92,7 @@
             n = 4 + 4 * c + b
             across.append(
                 remote(
-                    peram.at[c, 0, 1 - h, :, b * NEV : (b + 1) * NEV], taub.at[c, b, y, my_tau],
+                    peram.at[c, 0, 1 - h, :, b * NEV : (b + 1) * NEV], taub.at[y, c, b, my_tau],
                     bsend.at[n], brecv.at[n], sibling,
                 )
             )
@@ -102,8 +102,8 @@
     first, second = [], []
     for d in range(1, 4):
         y2, z2 = lax.rem(y + d, 4), lax.rem(z + d, 4)
-        first.append(remote(taub.at[:, :, y], taub.at[:, :, y], tsend.at[d - 1], trecv.at[d - 1], at(y2, z)))
-        second.append(remote(tout.at[d - 1], tsel.at[:, :, z], tsend.at[d + 2], trecv.at[d + 2], at(y, z2)))
+        first.append(remote(taub.at[y], taub.at[y], tsend.at[d - 1], trecv.at[d - 1], at(y2, z)))
+        second.append(remote(tout.at[d - 1], tsel.at[z], tsend.at[d + 2], trecv.at[d + 2], at(y, z2)))
 
     def spread_rows():
         for n in range(4, 12):
@@ -114,7 +114,7 @@
 
     def pick(d, n, c):
         target = y * 4 + lax.rem(z + d, 4)
-        return taub[c, spin_ref[n, pair_ref[0, target]], spin_ref[n, target]]
+        return taub[spin_ref[n, target], c, spin_ref[n, pair_ref[0, target]]]
 
     def spread_blocks():
         for copy in first:
@@ -126,7 +126,7 @@
             second[d - 1].start()
         for n in range(3):
             for c in range(2):
-                tsel[n, c, z] = pick(0, n, c)
+                tsel[z, n, c] = pick(0, n, c)
 
     def hand_on(slot, g):
         return remote(rown.at[slot], rnb.at[slot], xsend.at[slot], xrecv.at[slot], beside(g))
@@ -192,7 +192,7 @@
         copy.wait_recv()
 
     def block(c, n):
-        return tsel[n, c].reshape(NEV, NEV)
+        return jnp.concatenate([tsel[k, n, c] for k in range(4)], axis=0)
 
     third_re, third_im = block(0, 2), block(1, 2)
     t3m[...] = jnp.concatenate(
@@ -360,9 +360,9 @@
             pltpu.VMEM((30, NEV, 512), BF16),
             pltpu.VMEM((32, NEV, 512), BF16),
             pltpu.VMEM((32, NEV, 512), BF16),
-            pltpu.VMEM((2, 4, 4, 32, NEV), BF16),
+            pltpu.VMEM((4, 2, 4, 32, NEV), BF16),
             pltpu.VMEM((3, 3, 2, 32, NEV), BF16),
-            pltpu.VMEM((3, 2, 4, 32, NEV), BF16),
+            pltpu.VMEM((4, 3, 2, 32, NEV), BF16),
             pltpu.VMEM((2, 16 * NEV, NEV), F32),
             pltpu.VMEM((2 * NEV * NEV, NEV), F32),
             pltpu.VMEM((2 * NEV, 2 * NEV), F32),

time: 85 us -> 84.1 us (0.989)
  Pallas kernels: 83.6 us -> 82.7 us
where the time goes in v3:
time: 84.1 us; the launch traced here: 84 us
  Pallas kernels  82.7 us (98%)
  local copies, waits for them, and re-layouts  1.26 us (1%)
    pallas_call x1, Pallas kernels, on_device(): pl.pallas_call(kernel, name='correlate', out_shape=jax.ShapeDtypeStruct((...  82.7 us

profile of v3, /device:TPU:1, one launch (start us, length us, event | category | flops | bytes accessed | tf_op | source)
XLA Modules:
  0.0 84.0 jit_solution(12918092779915873836)
XLA Ops:
  0.0 82.7 %correlate.1 = f32[8,128]{1,0:T(8,128)} custom-call(s32[1,16]{1,0:T(1,128)} %bitcast.8, s32[3,16]{1,0:T(4,128)} %bitcast.7, bf16[2,1,64,16384]{3,2,1,0:T(8,128)(2,1)} %sink.1, bf16[2,2,16,128,512]{4,3,2,1,0:T(8,128)(2,1)} %bitcast.6, bf16[2,1,2,16,512]{4,3,2,1,0:T(8,128)(2,1)} %peram.1), custom_call_target="tpu_custom_call" | custom-call | tf_op jit(solution)/shard_map/correlate/pallas_call | solution.py:344
  82.7 1.3 %slice.3 = f32[4,16]{1,0:T(4,128)} slice(f32[8,128]{1,0:T(8,128)} %correlate.1), slice={[0:4], [0:16]} | slice | bytes 512 | tf_op jit(solution)/shard_map/slice | solution.py:390

commit v4 on v3

--- a/solution.py
+++ b/solution.py
@@ -363,8 +363,8 @@
             pltpu.VMEM((4, 2, 4, 32, NEV), BF16),
             pltpu.VMEM((3, 3, 2, 32, NEV), BF16),
             pltpu.VMEM((4, 3, 2, 32, NEV), BF16),
-            pltpu.VMEM((2, 16 * NEV, NEV), F32),
-            pltpu.VMEM((2 * NEV * NEV, NEV), F32),
+            pltpu.VMEM((2, 16 * NEV + 16, NEV), F32),
+            pltpu.VMEM((2 * NEV * NEV + 2 * NEV, NEV), F32),
             pltpu.VMEM((2 * NEV, 2 * NEV), F32),
             pltpu.VMEM((2 * NEV, 2 * NEV), BF16),
             pltpu.VMEM((2 * NEV, 2 * NEV), BF16),

time: 84.1 us -> 84.1 us (level)
  no operation moved by 1% of the time
where the time goes in v4:
time: 84.1 us; the launch traced here: 84 us
  Pallas kernels  82.7 us (98%)
  local copies, waits for them, and re-layouts  1.26 us (1%)
    pallas_call x1, Pallas kernels, on_device(): pl.pallas_call(kernel, name='correlate', out_shape=jax.ShapeDtypeStruct((...  82.7 us

profile of v4, /device:TPU:1, one launch (start us, length us, event | category | flops | bytes accessed | tf_op | source)
XLA Modules:
  0.0 84.0 jit_solution(12031866479256625674)
XLA Ops:
  0.0 82.7 %correlate.1 = f32[8,128]{1,0:T(8,128)} custom-call(s32[1,16]{1,0:T(1,128)} %bitcast.8, s32[3,16]{1,0:T(4,128)} %bitcast.7, bf16[2,1,64,16384]{3,2,1,0:T(8,128)(2,1)} %sink.1, bf16[2,2,16,128,512]{4,3,2,1,0:T(8,128)(2,1)} %bitcast.6, bf16[2,1,2,16,512]{4,3,2,1,0:T(8,128)(2,1)} %peram.1), custom_call_target="tpu_custom_call" | custom-call | tf_op jit(solution)/shard_map/correlate/pallas_call | solution.py:344
  82.7 1.3 %slice.3 = f32[4,16]{1,0:T(4,128)} slice(f32[8,128]{1,0:T(8,128)} %correlate.1), slice={[0:4], [0:16]} | slice | bytes 512 | tf_op jit(solution)/shard_map/slice | solution.py:390

commit v5 on v4

--- a/solution.py
+++ b/solution.py
@@ -283,15 +283,6 @@
 
     lax.fori_loop(0, 15, main, (orders, start))
 
-    for copy in across + first + second:
-        copy.wait_send()
-
-    def drain_sends(k, inner):
-        remote(sbuf.at[k], sbuf.at[k], ssem.at[k], xrecv.at[0], sibling).wait_send()
-        return inner
-
-    lax.fori_loop(0, 30, drain_sends, 0)
-
     first_re, first_im = block(0, 0).astype(F32), block(1, 0).astype(F32)
     fetched, given = pacc[:, :NEV], pacc[:, NEV:]
     with_re, with_im = jnp.where(par == 0, fetched, given), jnp.where(par == 0, given, fetched)
@@ -325,6 +316,15 @@
         return carry
 
     lax.fori_loop(0, 32, drain_hands, 0)
+
+    for copy in across + first + second:
+        copy.wait_send()
+
+    def drain_sends(k, inner):
+        remote(sbuf.at[k], sbuf.at[k], ssem.at[k], xrecv.at[0], sibling).wait_send()
+        return inner
+
+    lax.fori_loop(0, 30, drain_sends, 0)
 
     def share_wait(k, carry):
         who = lax.rem(chip + k, 16)

time: 84.1 us -> 83.9 us (level)
  no operation moved by 1% of the time
where the time goes in v5:
time: 83.9 us; the launch traced here: 83.8 us
  Pallas kernels  82.5 us (98%)
  local copies, waits for them, and re-layouts  1.26 us (2%)
    pallas_call x1, Pallas kernels, on_device(): pl.pallas_call(kernel, name='correlate', out_shape=jax.ShapeDtypeStruct((...  82.5 us

profile of v5, /device:TPU:1, one launch (start us, length us, event | category | flops | bytes accessed | tf_op | source)
XLA Modules:
  0.0 83.8 jit_solution(3440285178275280324)
XLA Ops:
  0.0 82.5 %correlate.1 = f32[8,128]{1,0:T(8,128)} custom-call(s32[1,16]{1,0:T(1,128)} %bitcast.8, s32[3,16]{1,0:T(4,128)} %bitcast.7, bf16[2,1,64,16384]{3,2,1,0:T(8,128)(2,1)} %sink.1, bf16[2,2,16,128,512]{4,3,2,1,0:T(8,128)(2,1)} %bitcast.6, bf16[2,1,2,16,512]{4,3,2,1,0:T(8,128)(2,1)} %peram.1), custom_call_target="tpu_custom_call" | custom-call | tf_op jit(solution)/shard_map/correlate/pallas_call | solution.py:344
  82.5 1.3 %slice.3 = f32[4,16]{1,0:T(4,128)} slice(f32[8,128]{1,0:T(8,128)} %correlate.1), slice={[0:4], [0:16]} | slice | bytes 512 | tf_op jit(solution)/shard_map/slice | solution.py:390
